TPU v7x, 32 devices: a whole 2x2x4 slice. The times are simulated.
32 devices in a mesh: energy: 4 (over z), rows: 8 (over y, x, core).
Axes of the slice: x: 2, y: 2, z: 4, core: 2. Of those that a mesh axis runs over, the one named last changes fastest.
Arguments:
- coupling: bfloat16 [2, 512, 512], replicated, may hold values from -4.1875 to 4.1875
- inverses: bfloat16 [32, 4, 2, 256, 256], P(('energy', 'rows')), may hold values from -0.0078125 to 0.0078125
- contact_row: int32 [12], replicated, may hold values from 0 to 7, as said below
- assignment: int32 [8], P('energy'), may hold values from 0 to 7, as said below
- states: bfloat16 [12, 2, 16, 512], replicated, may hold values from -0.119628906 to 0.119628906
- weights: float32 [8], P('energy'), may hold values from 0.03 to 0.3
Outputs:
- injection: float32 [8, 8, 2, 16, 512], P('energy', 'rows')
- integrated: float32 [8, 2, 16, 512], P('rows')
- far_forward: bfloat16 [32, 2, 256, 256], P(('energy', 'rows'))
- far_backward: bfloat16 [32, 2, 256, 256], P(('energy', 'rows'))
Inputs may be any that keep to these rules, and one draw needn't show every extreme that they name: `contact_row`: every device block row has one contact or more. `assignment`: each aligned block of 2 entries, b * 2 to b * 2 + 1, holds each of those same numbers once.
All inputs are finite; a program needn't handle non-finite values.
Results may differ from a plain program's by a relative error of at most 0.024.
Values may be sent and summed in bfloat16 or wider, within the bound.
A program may use at most 64 MiB of HBM per device.

v0:
```python
import jax
import jax.numpy as jnp
from jax import lax
from jax.sharding import PartitionSpec as P

ITERS = 4
ROWS_DEV = 1


def partner(shard, axis, stride):
    return lax.ppermute(shard, axis, [(i, i ^ 1 << stride) for i in range(lax.axis_size(axis))])


def single(leading, trailing):
    return jnp.dot(leading, trailing, preferred_element_type=jnp.float32)


def paired_dot(first_left, first_right, second_left, second_right):
    real_part = (
        single(first_left[0], first_right[0])
        - single(first_left[1], first_right[1])
        + single(second_left[0], second_right[0])
        - single(second_left[1], second_right[1])
    )
    imag_part = (
        single(first_left[0], first_right[1])
        + single(first_left[1], first_right[0])
        + single(second_left[0], second_right[1])
        + single(second_left[1], second_right[0])
    )
    return jnp.stack([real_part, imag_part])


def block_product(own_left, other_left, own_right, other_right, row_bit, column_bit):

    def aligned():
        return paired_dot(own_left, own_right, other_left, other_right)

    def crossed():
        return paired_dot(own_left, other_right, other_left, own_right)

    return lax.cond(row_bit == column_bit, aligned, crossed)


def quarter(matrix, row_half, column_half, half_order):
    return lax.dynamic_slice(
        matrix,
        (jnp.int32(0), row_half * half_order, column_half * half_order),
        (2, half_order, half_order),
    )


def local(coupling, inverses, contact_row, assignment, states, weights):
    position = lax.axis_index("rows")
    row_bit = position // 2 % 2
    column_bit = position % 2
    half_order = inverses.shape[-1]
    forward = quarter(coupling, row_bit, column_bit, half_order)
    mirror = quarter(coupling, column_bit, row_bit, half_order)
    backward = jnp.stack([mirror[0].T, -mirror[1].T])
    surface_sum = jnp.zeros((2, half_order, half_order), jnp.float32)
    for iteration in range(ITERS):
        inverse = inverses[0, iteration]
        forward_far, backward_far = partner((forward, backward), "rows", 0)
        inverse_down, forward_down, backward_down = partner((inverse, forward, backward), "rows", 1)
        forward_green = block_product(
            forward, forward_far, inverse, inverse_down, row_bit, column_bit
        ).astype(jnp.bfloat16)
        backward_green = block_product(
            backward, backward_far, inverse, inverse_down, row_bit, column_bit
        ).astype(jnp.bfloat16)
        forward_green_far, backward_green_far = partner((forward_green, backward_green), "rows", 0)
        surface_sum = surface_sum + block_product(
            forward_green, forward_green_far, backward, backward_down, row_bit, column_bit
        )
        forward_next = block_product(
            forward_green, forward_green_far, forward, forward_down, row_bit, column_bit
        ).astype(jnp.bfloat16)
        backward = block_product(
            backward_green, backward_green_far, backward, backward_down, row_bit, column_bit
        ).astype(jnp.bfloat16)
        forward = forward_next
    self_energy = surface_sum.astype(jnp.bfloat16)
    groups = assignment.shape[0]
    states_count = states.shape[2]
    contacts = contact_row.shape[0]
    flat_states = states.reshape(contacts, -1)
    block_rows = ROWS_DEV * lax.axis_size("rows")
    row_ids = jnp.arange(block_rows, dtype=jnp.int32)
    selector = (contact_row[None, :] == row_ids[:, None]).astype(jnp.bfloat16)
    drive = jnp.dot(selector, flat_states, preferred_element_type=jnp.float32).astype(jnp.bfloat16)
    drive = drive.reshape(block_rows, 2, states_count, 2, half_order)
    drive_half = lax.dynamic_index_in_dim(drive, column_bit, axis=3, keepdims=False)

    def contract_own(energy_part, drive_part):
        return jnp.einsum(
            "mn,rkn->rkm", energy_part, drive_part, preferred_element_type=jnp.float32
        )

    real_part = contract_own(self_energy[0], drive_half[:, 0]) - contract_own(
        self_energy[1], drive_half[:, 1]
    )
    imag_part = contract_own(self_energy[0], drive_half[:, 1]) + contract_own(
        self_energy[1], drive_half[:, 0]
    )
    partial_terms = jnp.stack([real_part, imag_part], axis=1)
    received = lax.all_to_all(
        partial_terms[:, None].astype(jnp.bfloat16), "rows", split_axis=0, concat_axis=1, tiled=True
    ).astype(jnp.float32)
    summed = received.reshape(ROWS_DEV, groups, 2, 2, 2, states_count, half_order).sum(axis=3)
    slots = summed.transpose(1, 0, 3, 4, 2, 5).reshape(
        groups, ROWS_DEV, 2, states_count, 2 * half_order
    )
    local_slot = assignment % groups
    slot_index = jnp.arange(groups, dtype=jnp.int32)
    source_slot = jnp.sum(
        jnp.where(local_slot[None, :] == slot_index[:, None], slot_index[None, :], 0), axis=1
    )
    injection = jnp.take(slots, source_slot, axis=0)
    weighted = jnp.tensordot(weights, injection, axes=1, precision=lax.Precision.HIGHEST)
    integrated = lax.psum(weighted.astype(jnp.bfloat16), "energy").astype(jnp.float32)
    return (injection, integrated, forward[None], backward[None])


def solution(mesh):
    placed = (
        P(),
        P(("energy", "rows"), None, None, None, None),
        P(),
        P("energy"),
        P(),
        P("energy"),
    )
    return jax.shard_map(
        local,
        mesh=mesh,
        in_specs=placed,
        out_specs=(
            P("energy", "rows", None, None, None),
            P("rows", None, None, None),
            P(("energy", "rows"), None, None, None),
            P(("energy", "rows"), None, None, None),
        ),
        check_vma=False,
    )
```

profile of v0, /device:TPU:0, one launch (start us, length us, event | category | flops | bytes accessed | tf_op | source)
XLA Modules:
  0.0 174.6 jit_solution(10024723884173628811)
XLA Ops:
  1.7 3.0 %collective-permute-start.4 = (bf16[2,256,256]{2,1,0:T(8,128)(2,1)S(1)}, bf16[2,256,256]{2,1,0:T(8,128)(2,1)S(1)}, u32[]{:S(2)}, u32[]{:S(2)}) collective-permute-start(bf16[2,256,256]{2,1,0:T(8,128)(2,1)S(1)} %constant_dynamic-slice_fusion.1), channel_id=1, source_target_pairs={{0,2},{1,3},{2,0},{3,1},{4,6},{5,7},{6,4},{7,5},{8,10},{9,11},{10,... | collective-permute-start | bytes 786440 | tf_op jit(solution)/shard_map/ppermute | solution.py:11
  7.9 8.7 %collective-permute-done = bf16[2,256,256]{2,1,0:T(8,128)(2,1)S(1)} collective-permute-done((bf16[2,256,256]{2,1,0:T(8,128)(2,1)S(1)}, bf16[2,256,256]{2,1,0:T(8,128)(2,1)S(1)}, u32[]{:S(2)}, u32[]{:S(2)}) %collective-permute-start) | collective-permute-done | bytes 262176 | tf_op jit(solution)/shard_map/ppermute | solution.py:11
  18.3 1.8 %collective-permute-start.2 = (bf16[2,256,256]{2,1,0:T(8,128)(2,1)S(1)}, bf16[2,256,256]{2,1,0:T(8,128)(2,1)}, u32[]{:S(2)}, u32[]{:S(2)}) collective-permute-start(bf16[2,256,256]{2,1,0:T(8,128)(2,1)S(1)} %pad_maximum_fusion.40), channel_id=1, source_target_pairs={{0,2},{1,3},{2,0},{3,1},{4,6},{5,7},{6,4},{7,5},{8,10},{9,11},{10,... | collective-permute-start | bytes 786440 | tf_op jit(solution)/shard_map/ppermute | solution.py:11
  27.6 5.2 %conditional.105 = (bf16[2,256,256]{2,1,0:T(8,128)(2,1)S(1)}) conditional(s32[]{:T(128)} %convert_element_type.223, (bf16[2,256,256]{2,1,0:T(8,128)(2,1)S(1)}, bf16[2,256,256]{2,1,0:T(8,128)(2,1)}, bf16[2,256,256]{2,1,0:T(8,128)(2,1)S(1)}, bf16[256,256]{1,0:T(8,128)(2,1)S(1)}, bf16[256,256]{1,0:T(8,128)(2,1)S(1)}) %tuple.379, ...), branch_computations={%region_11.12_spmd, %region_12.13_spmd} | conditional | flops 269090816 | bytes 6029320
  38.8 5.2 %conditional.107 = (bf16[2,256,256]{2,1,0:T(8,128)(2,1)S(1)}) conditional(s32[]{:T(128)} %convert_element_type.223, (bf16[2,256,256]{2,1,0:T(8,128)(2,1)S(1)}, bf16[2,256,256]{2,1,0:T(8,128)(2,1)}, bf16[2,256,256]{2,1,0:T(8,128)(2,1)S(1)}, bf16[2,256,256]{2,1,0:T(8,128)(2,1)S(1)}) %tuple.302, (bf16[2,256,256]{2,1,0:T(8,128)(2,1)S(1)}, ...), branch_computations={%region_15.16_spmd, %region_16.17_spmd} | conditional | flops 269090816 | bytes 6029320
  44.5 1.8 %collective-permute-start.18 = (bf16[2,256,256]{2,1,0:T(8,128)(2,1)S(1)}, bf16[2,256,256]{2,1,0:T(8,128)(2,1)}, u32[]{:S(2)}, u32[]{:S(2)}) collective-permute-start(bf16[2,256,256]{2,1,0:T(8,128)(2,1)S(1)} %get-tuple-element.685), channel_id=1, source_target_pairs={{0,2},{1,3},{2,0},{3,1},{4,6},{5,7},{6,4},{7,5},{8,10},{9,11},{10,... | collective-permute-start | bytes 786440 | tf_op jit(solution)/shard_map/ppermute | solution.py:11
  46.3 3.7 %collective-permute-done.9 = bf16[2,256,256]{2,1,0:T(8,128)(2,1)} collective-permute-done((bf16[2,256,256]{2,1,0:T(8,128)(2,1)S(1)}, bf16[2,256,256]{2,1,0:T(8,128)(2,1)}, u32[]{:S(2)}, u32[]{:S(2)}) %collective-permute-start.9) | collective-permute-done | bytes 262176 | tf_op jit(solution)/shard_map/ppermute | solution.py:11
  50.0 5.2 %conditional.110 = (bf16[2,256,256]{2,1,0:T(8,128)(2,1)S(1)}) conditional(s32[]{:T(128)} %convert_element_type.223, (bf16[2,256,256]{2,1,0:T(8,128)(2,1)S(1)}, bf16[2,256,256]{2,1,0:T(8,128)(2,1)}, bf16[2,256,256]{2,1,0:T(8,128)(2,1)S(1)}, bf16[2,256,256]{2,1,0:T(8,128)(2,1)S(1)}) %tuple.308, (bf16[2,256,256]{2,1,0:T(8,128)(2,1)S(1)}, ...), branch_computations={%region_21.22_spmd, %region_22.23_spmd} | conditional | flops 269090816 | bytes 6029320
  55.3 5.4 %conditional.108 = (bf16[2,256,256]{2,1,0:T(8,128)(2,1)S(1)}) conditional(s32[]{:T(128)} %convert_element_type.223, (bf16[2,256,256]{2,1,0:T(8,128)(2,1)S(1)}, bf16[2,256,256]{2,1,0:T(8,128)(2,1)S(1)}, bf16[2,256,256]{2,1,0:T(8,128)(2,1)}, bf16[2,256,256]{2,1,0:T(8,128)(2,1)S(1)}) %tuple.304, (bf16[2,256,256]{2,1,0:T(8,128)(2,1)S(1)}, ...), branch_computations={%region_17.18_spmd, %region_18.19_spmd} | conditional | flops 269090816 | bytes 6029320
  65.6 2.0 %convolution_convert_fusion = bf16[8,16384]{1,0:T(8,128)(2,1)} fusion(bf16[12,16384]{1,0:T(8,128)(2,1)} %bitcast.1814, s32[12]{0:T(128)S(1)} %copy-done.4), kind=kOutput, calls=%fused_computation.1673 | convolution fusion | flops 3276896 | bytes 655408 | tf_op jit(solution)/shard_map/dot_general | solution.py:91
  68.0 5.9 %conditional.114 = (bf16[2,256,256]{2,1,0:T(8,128)(2,1)}) conditional(s32[]{:T(128)} %convert_element_type.223, (bf16[2,256,256]{2,1,0:T(8,128)(2,1)S(1)}, bf16[2,256,256]{2,1,0:T(8,128)(2,1)S(1)}, bf16[2,256,256]{2,1,0:T(8,128)(2,1)}, bf16[2,256,256]{2,1,0:T(8,128)(2,1)S(1)}) %tuple.316, (bf16[2,256,256]{2,1,0:T(8,128)(2,1)S(1)}, ...), branch_computations={%region_29.30_spmd, %region_30.31_spmd} | conditional | flops 269090816 | bytes 6029320
  73.9 5.5 %conditional.112 = (bf16[2,256,256]{2,1,0:T(8,128)(2,1)S(1)}) conditional(s32[]{:T(128)} %convert_element_type.223, (bf16[2,256,256]{2,1,0:T(8,128)(2,1)S(1)}, bf16[2,256,256]{2,1,0:T(8,128)(2,1)}, bf16[2,256,256]{2,1,0:T(8,128)(2,1)}, bf16[2,256,256]{2,1,0:T(8,128)(2,1)S(1)}) %tuple.312, (bf16[2,256,256]{2,1,0:T(8,128)(2,1)S(1)}, ...), branch_computations={%region_25.26_spmd, %region_26.27_spmd} | conditional | flops 269090816 | bytes 6029320
  79.3 3.9 %collective-permute-start.20 = (bf16[2,256,256]{2,1,0:T(8,128)(2,1)S(1)}, bf16[2,256,256]{2,1,0:T(8,128)(2,1)S(1)}, u32[]{:S(2)}, u32[]{:S(2)}) collective-permute-start(bf16[2,256,256]{2,1,0:T(8,128)(2,1)S(1)} %get-tuple-element.690), channel_id=1, source_target_pairs={{0,1},{1,0},{2,3},{3,2},{4,5},{5,4},{6,7},{7,6},{8,9},{9,8},{10,11... | collective-permute-start | bytes 786440 | tf_op jit(solution)/shard_map/ppermute | solution.py:11
  84.9 9.1 %conditional.115 = (bf16[2,256,256]{2,1,0:T(8,128)(2,1)S(1)}) conditional(s32[]{:T(128)} %convert_element_type.223, (bf16[2,256,256]{2,1,0:T(8,128)(2,1)}, bf16[2,256,256]{2,1,0:T(8,128)(2,1)}, bf16[2,256,256]{2,1,0:T(8,128)(2,1)}, bf16[2,256,256]{2,1,0:T(8,128)(2,1)S(1)}) %tuple.318, (bf16[2,256,256]{2,1,0:T(8,128)(2,1)}, ...), branch_computations={%region_31.32_spmd, %region_32.33_spmd} | conditional | flops 269090816 | bytes 6029320
  98.4 5.2 %conditional.101 = (f32[2,256,256]{2,1,0:T(8,128)S(1)}) conditional(s32[]{:T(128)} %convert_element_type.223, (bf16[2,256,256]{2,1,0:T(8,128)(2,1)S(1)}, bf16[2,256,256]{2,1,0:T(8,128)(2,1)}, bf16[2,256,256]{2,1,0:T(8,128)(2,1)S(1)}, bf16[256,256]{1,0:T(8,128)(2,1)S(1)}, bf16[256,256]{1,0:T(8,128)(2,1)S(1)}) %tuple.381, ...), branch_computations={%region_3.4_spmd, %region_4.5_spmd} | conditional | flops 268959744 | bytes 6815752 | solution.py:42
  103.6 5.2 %conditional.106 = (f32[2,256,256]{2,1,0:T(8,128)S(1)}) conditional(s32[]{:T(128)} %convert_element_type.223, (bf16[2,256,256]{2,1,0:T(8,128)(2,1)S(1)}, bf16[2,256,256]{2,1,0:T(8,128)(2,1)}, bf16[2,256,256]{2,1,0:T(8,128)(2,1)S(1)}, bf16[2,256,256]{2,1,0:T(8,128)(2,1)S(1)}) %tuple.300, (bf16[2,256,256]{2,1,0:T(8,128)(2,1)S(1)}, ...), branch_computations={%region_13.14_spmd, %region_14.15_spmd} | conditional | flops 268959744 | bytes 6815752 | solution.py:42
  109.5 6.3 %conditional.111 = (f32[2,256,256]{2,1,0:T(8,128)}) conditional(s32[]{:T(128)} %convert_element_type.223, (bf16[2,256,256]{2,1,0:T(8,128)(2,1)S(1)}, bf16[2,256,256]{2,1,0:T(8,128)(2,1)}, bf16[2,256,256]{2,1,0:T(8,128)(2,1)}, bf16[2,256,256]{2,1,0:T(8,128)(2,1)S(1)}) %tuple.310, (bf16[2,256,256]{2,1,0:T(8,128)(2,1)S(1)}, ...), branch_computations={%region_23.24_spmd, %region_24.25_spmd} | conditional | flops 268959744 | bytes 6815752 | solution.py:42
  115.8 5.2 %conditional.118 = (bf16[2,256,256]{2,1,0:T(8,128)(2,1)S(1)}) conditional(s32[]{:T(128)} %convert_element_type.223, (bf16[2,256,256]{2,1,0:T(8,128)(2,1)S(1)}, bf16[2,256,256]{2,1,0:T(8,128)(2,1)S(1)}, bf16[2,256,256]{2,1,0:T(8,128)(2,1)}, bf16[2,256,256]{2,1,0:T(8,128)(2,1)S(1)}) %tuple.324, (bf16[2,256,256]{2,1,0:T(8,128)(2,1)S(1)}, ...), branch_computations={%region_39.40_spmd, %region_40.41_spmd} | conditional | flops 269090816 | bytes 6029320
  121.0 3.5 %collective-permute-start.27 = (bf16[2,256,256]{2,1,0:T(8,128)(2,1)S(1)}, bf16[2,256,256]{2,1,0:T(8,128)(2,1)S(1)}, u32[]{:S(2)}, u32[]{:S(2)}) collective-permute-start(bf16[2,256,256]{2,1,0:T(8,128)(2,1)S(1)} %get-tuple-element.696), channel_id=1, source_target_pairs={{0,1},{1,0},{2,3},{3,2},{4,5},{5,4},{6,7},{7,6},{8,9},{9,8},{10,11... | collective-permute-start | bytes 786440 | tf_op jit(solution)/shard_map/ppermute | solution.py:11
  124.5 6.5 %conditional.116 = (f32[2,256,256]{2,1,0:T(8,128)}) conditional(s32[]{:T(128)} %convert_element_type.223, (bf16[2,256,256]{2,1,0:T(8,128)(2,1)S(1)}, bf16[2,256,256]{2,1,0:T(8,128)(2,1)}, bf16[2,256,256]{2,1,0:T(8,128)(2,1)}, bf16[2,256,256]{2,1,0:T(8,128)(2,1)S(1)}) %tuple.320, (bf16[2,256,256]{2,1,0:T(8,128)(2,1)S(1)}, ...), branch_computations={%region_33.34_spmd, %region_34.35_spmd} | conditional | flops 268959744 | bytes 6815752 | solution.py:42
  133.7 6.9 %all-to-all-start = ((bf16[8,1,2,16,256]{4,3,2,1,0:T(8,128)(2,1)}), bf16[8,1,2,16,256]{4,3,2,1,0:T(8,128)(2,1)S(1)}, u32[]{:S(2)}, u32[]{:S(2)}) async-start(bf16[8,1,2,16,256]{4,3,2,1,0:T(8,128)(2,1)} %copy.23), calls=%async_computation | async-start | bytes 262144 | tf_op jit(solution)/shard_map/all_to_all | solution.py:107
  140.6 5.2 %conditional.117 = (bf16[1,2,256,256]{3,2,1,0:T(8,128)(2,1)S(1)}) conditional(s32[]{:T(128)} %convert_element_type.223, (bf16[2,256,256]{2,1,0:T(8,128)(2,1)S(1)}, bf16[2,256,256]{2,1,0:T(8,128)(2,1)S(1)}, bf16[2,256,256]{2,1,0:T(8,128)(2,1)}, bf16[2,256,256]{2,1,0:T(8,128)(2,1)S(1)}) %tuple.322, (bf16[2,256,256]{2,1,0:T(8,128)(2,1)S(1)}, ...), branch_computations={%region_37.38_spmd, %region_38.39_spmd} | conditional | flops 269090816 | bytes 6029320
  146.5 5.2 %conditional.119 = (bf16[1,2,256,256]{3,2,1,0:T(8,128)(2,1)S(1)}) conditional(s32[]{:T(128)} %convert_element_type.223, (bf16[2,256,256]{2,1,0:T(8,128)(2,1)S(1)}, bf16[2,256,256]{2,1,0:T(8,128)(2,1)}, bf16[2,256,256]{2,1,0:T(8,128)(2,1)S(1)}, bf16[2,256,256]{2,1,0:T(8,128)(2,1)S(1)}) %tuple.326, (bf16[2,256,256]{2,1,0:T(8,128)(2,1)S(1)}, ...), branch_computations={%region_41.42_spmd, %region_42.43_spmd} | conditional | flops 269090816 | bytes 6029320
  154.7 19.3 %psum.7 = bf16[1,2,16,512]{3,2,1,0:T(8,128)(2,1)S(1)} all-reduce(bf16[1,2,16,512]{3,2,1,0:T(8,128)(2,1)S(1)} %copy.44), channel_id=1, replica_groups=mesh['energy'=4,'rows'=8] {'energy'}, use_global_device_ids=true, to_apply=%region_36.37 | all-reduce | flops 16384 | bytes 65536 | tf_op jit(solution)/shard_map/psum | solution.py:121
  (281 shorter events, 126.6 us)
Async XLA Ops:
  1.7 20.4 %collective-permute-start.4 = (bf16[2,256,256]{2,1,0:T(8,128)(2,1)S(1)}, bf16[2,256,256]{2,1,0:T(8,128)(2,1)S(1)}, u32[]{:S(2)}, u32[]{:S(2)}) collective-permute-start(bf16[2,256,256]{2,1,0:T(8,128)(2,1)S(1)} %constant_dynamic-slice_fusion.1), channel_id=1, source_target_pairs={{0,2},{1,3},{2,0},{3,1},{4,6},{5,7},{6,4},{7,5},{8,10},{9,11},{10,... | collective-permute-start | bytes 786440 | tf_op jit(solution)/shard_map/ppermute | solution.py:11
  6.0 10.7 %collective-permute-start = (bf16[2,256,256]{2,1,0:T(8,128)(2,1)S(1)}, bf16[2,256,256]{2,1,0:T(8,128)(2,1)S(1)}, u32[]{:S(2)}, u32[]{:S(2)}) collective-permute-start(bf16[2,256,256]{2,1,0:T(8,128)(2,1)S(1)} %get-tuple-element.674), channel_id=1, source_target_pairs={{0,2},{1,3},{2,0},{3,1},{4,6},{5,7},{6,4},{7,5},{8,10},{9,11},{10,... | collective-permute-start | bytes 786440 | tf_op jit(solution)/shard_map/ppermute | solution.py:11
  7.4 13.0 %collective-permute-start.7 = (bf16[2,256,256]{2,1,0:T(8,128)(2,1)S(1)}, bf16[2,256,256]{2,1,0:T(8,128)(2,1)S(1)}, u32[]{:S(2)}, u32[]{:S(2)}) collective-permute-start(bf16[2,256,256]{2,1,0:T(8,128)(2,1)S(1)} %pad_maximum_fusion.40), channel_id=1, source_target_pairs={{0,1},{1,0},{2,3},{3,2},{4,5},{5,4},{6,7},{7,6},{8,9},{9,8},{10,11... | collective-permute-start | bytes 786440 | tf_op jit(solution)/shard_map/ppermute | solution.py:11
  18.3 9.3 %collective-permute-start.2 = (bf16[2,256,256]{2,1,0:T(8,128)(2,1)S(1)}, bf16[2,256,256]{2,1,0:T(8,128)(2,1)}, u32[]{:S(2)}, u32[]{:S(2)}) collective-permute-start(bf16[2,256,256]{2,1,0:T(8,128)(2,1)S(1)} %pad_maximum_fusion.40), channel_id=1, source_target_pairs={{0,2},{1,3},{2,0},{3,1},{4,6},{5,7},{6,4},{7,5},{8,10},{9,11},{10,... | collective-permute-start | bytes 786440 | tf_op jit(solution)/shard_map/ppermute | solution.py:11
  20.1 13.0 %collective-permute-start.5 = (bf16[2,256,256]{2,1,0:T(8,128)(2,1)S(1)}, bf16[2,256,256]{2,1,0:T(8,128)(2,1)S(1)}, u32[]{:S(2)}, u32[]{:S(2)}) collective-permute-start(bf16[2,256,256]{2,1,0:T(8,128)(2,1)S(1)} %get-tuple-element.673), channel_id=1, source_target_pairs={{0,2},{1,3},{2,0},{3,1},{4,6},{5,7},{6,4},{7,5},{8,10},{9,11},{10,... | collective-permute-start | bytes 786440 | tf_op jit(solution)/shard_map/ppermute | solution.py:11
  23.7 9.5 %collective-permute-start.6 = (bf16[2,256,256]{2,1,0:T(8,128)(2,1)S(1)}, bf16[2,256,256]{2,1,0:T(8,128)(2,1)S(1)}, u32[]{:S(2)}, u32[]{:S(2)}) collective-permute-start(bf16[2,256,256]{2,1,0:T(8,128)(2,1)S(1)} %get-tuple-element.680), channel_id=1, source_target_pairs={{0,1},{1,0},{2,3},{3,2},{4,5},{5,4},{6,7},{7,6},{8,9},{9,8},{10,11... | collective-permute-start | bytes 786440 | tf_op jit(solution)/shard_map/ppermute | solution.py:11
  24.2 14.6 %collective-permute-start.11 = (bf16[2,256,256]{2,1,0:T(8,128)(2,1)S(1)}, bf16[2,256,256]{2,1,0:T(8,128)(2,1)}, u32[]{:S(2)}, u32[]{:S(2)}) collective-permute-start(bf16[2,256,256]{2,1,0:T(8,128)(2,1)S(1)} %get-tuple-element.680), channel_id=1, source_target_pairs={{0,2},{1,3},{2,0},{3,1},{4,6},{5,7},{6,4},{7,5},{8,10},{9,11},{10,... | collective-permute-start | bytes 786440 | tf_op jit(solution)/shard_map/ppermute | solution.py:11
  35.1 20.2 %collective-permute-start.12 = (bf16[2,256,256]{2,1,0:T(8,128)(2,1)S(1)}, bf16[2,256,256]{2,1,0:T(8,128)(2,1)S(1)}, u32[]{:S(2)}, u32[]{:S(2)}) collective-permute-start(bf16[2,256,256]{2,1,0:T(8,128)(2,1)S(1)} %get-tuple-element.675), channel_id=1, source_target_pairs={{0,2},{1,3},{2,0},{3,1},{4,6},{5,7},{6,4},{7,5},{8,10},{9,11},{10,... | collective-permute-start | bytes 786440 | tf_op jit(solution)/shard_map/ppermute | solution.py:11
  36.8 13.1 %collective-permute-start.9 = (bf16[2,256,256]{2,1,0:T(8,128)(2,1)S(1)}, bf16[2,256,256]{2,1,0:T(8,128)(2,1)}, u32[]{:S(2)}, u32[]{:S(2)}) collective-permute-start(bf16[2,256,256]{2,1,0:T(8,128)(2,1)S(1)} %get-tuple-element.683), channel_id=1, source_target_pairs={{0,2},{1,3},{2,0},{3,1},{4,6},{5,7},{6,4},{7,5},{8,10},{9,11},{10,... | collective-permute-start | bytes 786440 | tf_op jit(solution)/shard_map/ppermute | solution.py:11
  38.7 11.3 %collective-permute-start.15 = (bf16[2,256,256]{2,1,0:T(8,128)(2,1)S(1)}, bf16[2,256,256]{2,1,0:T(8,128)(2,1)S(1)}, u32[]{:S(2)}, u32[]{:S(2)}) collective-permute-start(bf16[2,256,256]{2,1,0:T(8,128)(2,1)S(1)} %get-tuple-element.687), channel_id=1, source_target_pairs={{0,1},{1,0},{2,3},{3,2},{4,5},{5,4},{6,7},{7,6},{8,9},{9,8},{10,11... | collective-permute-start | bytes 786440 | tf_op jit(solution)/shard_map/ppermute | solution.py:11
  44.0 11.3 %collective-permute-start.13 = (bf16[2,256,256]{2,1,0:T(8,128)(2,1)S(1)}, bf16[2,256,256]{2,1,0:T(8,128)(2,1)}, u32[]{:S(2)}, u32[]{:S(2)}) collective-permute-start(bf16[2,256,256]{2,1,0:T(8,128)(2,1)S(1)} %get-tuple-element.685), channel_id=1, source_target_pairs={{0,1},{1,0},{2,3},{3,2},{4,5},{5,4},{6,7},{7,6},{8,9},{9,8},{10,11... | collective-permute-start | bytes 786440 | tf_op jit(solution)/shard_map/ppermute | solution.py:11
  44.5 29.3 %collective-permute-start.18 = (bf16[2,256,256]{2,1,0:T(8,128)(2,1)S(1)}, bf16[2,256,256]{2,1,0:T(8,128)(2,1)}, u32[]{:S(2)}, u32[]{:S(2)}) collective-permute-start(bf16[2,256,256]{2,1,0:T(8,128)(2,1)S(1)} %get-tuple-element.685), channel_id=1, source_target_pairs={{0,2},{1,3},{2,0},{3,1},{4,6},{5,7},{6,4},{7,5},{8,10},{9,11},{10,... | collective-permute-start | bytes 786440 | tf_op jit(solution)/shard_map/ppermute | solution.py:11
  55.2 12.8 %collective-permute-start.21 = (bf16[2,256,256]{2,1,0:T(8,128)(2,1)S(1)}, bf16[2,256,256]{2,1,0:T(8,128)(2,1)}, u32[]{:S(2)}, u32[]{:S(2)}) collective-permute-start(bf16[2,256,256]{2,1,0:T(8,128)(2,1)S(1)} %get-tuple-element.688), channel_id=1, source_target_pairs={{0,1},{1,0},{2,3},{3,2},{4,5},{5,4},{6,7},{7,6},{8,9},{9,8},{10,11... | collective-permute-start | bytes 786440 | tf_op jit(solution)/shard_map/ppermute | solution.py:11
  60.7 13.2 %collective-permute-start.17 = (bf16[2,256,256]{2,1,0:T(8,128)(2,1)S(1)}, bf16[2,256,256]{2,1,0:T(8,128)(2,1)}, u32[]{:S(2)}, u32[]{:S(2)}) collective-permute-start(bf16[2,256,256]{2,1,0:T(8,128)(2,1)S(1)} %get-tuple-element.686), channel_id=1, source_target_pairs={{0,1},{1,0},{2,3},{3,2},{4,5},{5,4},{6,7},{7,6},{8,9},{9,8},{10,11... | collective-permute-start | bytes 786440 | tf_op jit(solution)/shard_map/ppermute | solution.py:11
  61.2 34.4 %collective-permute-start.19 = (bf16[2,256,256]{2,1,0:T(8,128)(2,1)S(1)}, bf16[2,256,256]{2,1,0:T(8,128)(2,1)S(1)}, u32[]{:S(2)}, u32[]{:S(2)}) collective-permute-start(bf16[2,256,256]{2,1,0:T(8,128)(2,1)S(1)} %get-tuple-element.672), channel_id=1, source_target_pairs={{0,2},{1,3},{2,0},{3,1},{4,6},{5,7},{6,4},{7,5},{8,10},{9,11},{10,... | collective-permute-start | bytes 786440 | tf_op jit(solution)/shard_map/ppermute | solution.py:11
  67.5 17.3 %collective-permute-start.16 = (bf16[2,256,256]{2,1,0:T(8,128)(2,1)S(1)}, bf16[2,256,256]{2,1,0:T(8,128)(2,1)}, u32[]{:S(2)}, u32[]{:S(2)}) collective-permute-start(bf16[2,256,256]{2,1,0:T(8,128)(2,1)S(1)} %get-tuple-element.688), channel_id=1, source_target_pairs={{0,2},{1,3},{2,0},{3,1},{4,6},{5,7},{6,4},{7,5},{8,10},{9,11},{10,... | collective-permute-start | bytes 786440 | tf_op jit(solution)/shard_map/ppermute | solution.py:11
  73.9 11.0 %collective-permute-start.22 = (bf16[2,256,256]{2,1,0:T(8,128)(2,1)}, bf16[2,256,256]{2,1,0:T(8,128)(2,1)}, u32[]{:S(2)}, u32[]{:S(2)}) collective-permute-start(bf16[2,256,256]{2,1,0:T(8,128)(2,1)} %get-tuple-element.692), channel_id=1, source_target_pairs={{0,1},{1,0},{2,3},{3,2},{4,5},{5,4},{6,7},{7,6},{8,9},{9,8},{10,11... | collective-permute-start | bytes 786440 | tf_op jit(solution)/shard_map/ppermute | solution.py:11
  79.3 16.3 %collective-permute-start.20 = (bf16[2,256,256]{2,1,0:T(8,128)(2,1)S(1)}, bf16[2,256,256]{2,1,0:T(8,128)(2,1)S(1)}, u32[]{:S(2)}, u32[]{:S(2)}) collective-permute-start(bf16[2,256,256]{2,1,0:T(8,128)(2,1)S(1)} %get-tuple-element.690), channel_id=1, source_target_pairs={{0,1},{1,0},{2,3},{3,2},{4,5},{5,4},{6,7},{7,6},{8,9},{9,8},{10,11... | collective-permute-start | bytes 786440 | tf_op jit(solution)/shard_map/ppermute | solution.py:11
  94.0 21.8 %collective-permute-start.26 = (bf16[2,256,256]{2,1,0:T(8,128)(2,1)S(1)}, bf16[2,256,256]{2,1,0:T(8,128)(2,1)}, u32[]{:S(2)}, u32[]{:S(2)}) collective-permute-start(bf16[2,256,256]{2,1,0:T(8,128)(2,1)S(1)} %get-tuple-element.693), channel_id=1, source_target_pairs={{0,1},{1,0},{2,3},{3,2},{4,5},{5,4},{6,7},{7,6},{8,9},{9,8},{10,11... | collective-permute-start | bytes 786440 | tf_op jit(solution)/shard_map/ppermute | solution.py:11
  94.1 30.4 %collective-permute-start.23 = (bf16[2,256,256]{2,1,0:T(8,128)(2,1)S(1)}, bf16[2,256,256]{2,1,0:T(8,128)(2,1)}, u32[]{:S(2)}, u32[]{:S(2)}) collective-permute-start(bf16[2,256,256]{2,1,0:T(8,128)(2,1)S(1)} %get-tuple-element.693), channel_id=1, source_target_pairs={{0,2},{1,3},{2,0},{3,1},{4,6},{5,7},{6,4},{7,5},{8,10},{9,11},{10,... | collective-permute-start | bytes 786440 | tf_op jit(solution)/shard_map/ppermute | solution.py:11
  97.2 27.3 %collective-permute-start.24 = (bf16[2,256,256]{2,1,0:T(8,128)(2,1)S(1)}, bf16[2,256,256]{2,1,0:T(8,128)(2,1)}, u32[]{:S(2)}, u32[]{:S(2)}) collective-permute-start(bf16[2,256,256]{2,1,0:T(8,128)(2,1)S(1)} %get-tuple-element.691), channel_id=1, source_target_pairs={{0,1},{1,0},{2,3},{3,2},{4,5},{5,4},{6,7},{7,6},{8,9},{9,8},{10,11... | collective-permute-start | bytes 786440 | tf_op jit(solution)/shard_map/ppermute | solution.py:11
  108.8 31.8 %collective-permute-start.25 = (bf16[2,256,256]{2,1,0:T(8,128)(2,1)S(1)}, bf16[2,256,256]{2,1,0:T(8,128)(2,1)S(1)}, u32[]{:S(2)}, u32[]{:S(2)}) collective-permute-start(bf16[2,256,256]{2,1,0:T(8,128)(2,1)S(1)} %get-tuple-element.690), channel_id=1, source_target_pairs={{0,2},{1,3},{2,0},{3,1},{4,6},{5,7},{6,4},{7,5},{8,10},{9,11},{10,... | collective-permute-start | bytes 786440 | tf_op jit(solution)/shard_map/ppermute | solution.py:11
  121.0 24.9 %collective-permute-start.27 = (bf16[2,256,256]{2,1,0:T(8,128)(2,1)S(1)}, bf16[2,256,256]{2,1,0:T(8,128)(2,1)S(1)}, u32[]{:S(2)}, u32[]{:S(2)}) collective-permute-start(bf16[2,256,256]{2,1,0:T(8,128)(2,1)S(1)} %get-tuple-element.696), channel_id=1, source_target_pairs={{0,1},{1,0},{2,3},{3,2},{4,5},{5,4},{6,7},{7,6},{8,9},{9,8},{10,11... | collective-permute-start | bytes 786440 | tf_op jit(solution)/shard_map/ppermute | solution.py:11
  133.7 18.0 %all-to-all-start = ((bf16[8,1,2,16,256]{4,3,2,1,0:T(8,128)(2,1)}), bf16[8,1,2,16,256]{4,3,2,1,0:T(8,128)(2,1)S(1)}, u32[]{:S(2)}, u32[]{:S(2)}) async-start(bf16[8,1,2,16,256]{4,3,2,1,0:T(8,128)(2,1)} %copy.23), calls=%async_computation | async-start | bytes 262144 | tf_op jit(solution)/shard_map/all_to_all | solution.py:107
  (11 other events, 184.6 us)
where the time goes:
time: 176 us; the launch traced here: 175 us
  matrix products  88.4 us (50%)
  starting transfers between devices  32.4 us (18%)
  blocking collectives  19.3 us (11%)
  waiting for transfers between devices  14.4 us (8%)
  local copies, waits for them, and re-layouts  11.5 us (7%)
  other arithmetic  5.75 us (3%)
    dot_general x160, matrix products, single(): return jnp.dot(leading, trailing, preferred_element_type=jnp.float32)  85 us
    ppermute x28, starting transfers between devices, partner(): lax.ppermute(shard, axis, [(i, i ^ 1 << stride) for i in range(lax.axis_s...  25.5 us
    psum x1, blocking collectives, local(): lax.psum(weighted.astype(jnp.bfloat16), 'energy').astype(jnp.float32)  19.3 us
    ppermute x28, waiting for transfers between devices, partner(): lax.ppermute(shard, axis, [(i, i ^ 1 << stride) for i in range(lax.axis_s...  14.4 us
    all_to_all x1, starting transfers between devices, local(): lax.all_to_all(partial_terms[:, None].astype(jnp.bfloat16), 'rows', split...  6.89 us
    unnamed x17, local copies, waits for them, and re-layouts  4.34 us
  transfers between devices with their start and end apart: 29, of which 4 were waited for; matrix products, arithmetic and copies ran while one was open for 57% of the time, Pallas kernels for 0%

commit v1 on v0

v1 whole, which is shorter than its diff:
```python
import functools

import jax
import jax.numpy as jnp
from jax import lax
from jax.experimental import pallas as pl
from jax.experimental.pallas import tpu as pltpu
from jax.sharding import PartitionSpec as P

MESH = pl.DeviceIdType.MESH
BF16 = jnp.bfloat16
F32 = jnp.float32


def remote(src, dst, send_sem, recv_sem, axis, target):
    return pltpu.make_async_remote_copy(
        src_ref=src,
        dst_ref=dst,
        send_sem=send_sem,
        recv_sem=recv_sem,
        device_id={axis: target},
        device_id_type=MESH,
    )


def mul(left, right):
    return jnp.dot(left, right, preferred_element_type=F32)


def kernel(
    rows_size,
    energy_size,
    coupling_ref,
    inverses_ref,
    contact_ref,
    assignment_ref,
    states_ref,
    weights_ref,
    injection_ref,
    integrated_ref,
    far_forward_ref,
    far_backward_ref,
    held,
    blocks,
    chain,
    product,
    right_chain,
    right_green,
    arrived,
    surface,
    drive,
    pieces,
    gathered,
    weighted,
    over_energy,
    stage,
    local_sems,
    cross_sems,
    core_sems,
    relay_sems,
    product_sems,
    far_sems,
    piece_send,
    piece_recv,
    energy_send,
    energy_recv,
):
    energy = lax.axis_index("energy")
    position = lax.axis_index("rows")
    iters = inverses_ref.shape[1]
    half = inverses_ref.shape[-1]
    whole = 2 * half
    groups = assignment_ref.shape[0]
    contacts, _, states_count, _ = states_ref.shape
    slot = position // 4
    row_bit = position // 2 % 2
    column_bit = position % 2
    across = slot * 4 + 2 * (1 - row_bit) + column_bit
    beside = slot * 4 + 2 * row_bit + 1 - column_bit
    own_block = 2 * row_bit + column_bit
    cross_block = 2 * (1 - row_bit) + column_bit

    load_coupling = pltpu.make_async_copy(coupling_ref, held, local_sems.at[0])
    load_coupling.start()
    load_inverse = pltpu.make_async_copy(
        inverses_ref.at[0], blocks.at[own_block], local_sems.at[1]
    )
    load_inverse.start()

    barrier = pltpu.get_barrier_semaphore()
    for step in range(1, rows_size):
        pl.semaphore_signal(
            barrier,
            inc=1,
            device_id={"rows": lax.rem(position + step, rows_size)},
            device_id_type=MESH,
        )
    for step in range(1, energy_size):
        pl.semaphore_signal(
            barrier,
            inc=1,
            device_id={"energy": lax.rem(energy + step, energy_size)},
            device_id_type=MESH,
        )
    pl.semaphore_wait(barrier, rows_size + energy_size - 2)

    cross = [
        remote(
            inverses_ref.at[0, k],
            blocks.at[own_block, k],
            cross_sems.at[0, k],
            cross_sems.at[1, k],
            "rows",
            across,
        )
        for k in range(iters)
    ]
    core = [
        remote(
            inverses_ref.at[0, k],
            blocks.at[own_block, k],
            core_sems.at[0, k],
            core_sems.at[1, k],
            "rows",
            beside,
        )
        for k in range(iters)
    ]
    relay = [
        remote(
            blocks.at[cross_block, k],
            blocks.at[cross_block, k],
            relay_sems.at[0, k],
            relay_sems.at[1, k],
            "rows",
            beside,
        )
        for k in range(iters)
    ]
    strip = pl.ds(pl.multiple_of(row_bit * half, half), half)
    share = [
        remote(
            product.at[k, strip],
            arrived.at[k],
            product_sems.at[0, k],
            product_sems.at[1, k],
            "rows",
            beside,
        )
        for k in range(iters)
    ]
    for k in range(iters):
        cross[k].start()
    for k in range(min(2, iters)):
        core[k].start()

    load_coupling.wait()

    def spread(part, index):
        for block in range(2):
            chain[:, pl.ds(block * whole + index * half, half)] = part[
                :, block * half : (block + 1) * half
            ]

    @pl.when(column_bit == 0)
    def _():
        spread(held[0], 0)
        spread(held[1], 1)

    @pl.when(column_bit == 1)
    def _():
        spread(held[0].T, 0)
        spread(-(held[1].T), 1)

    def build_chain(k):
        for block in range(2):
            for line in range(2):
                lines = slice(line * half, (line + 1) * half)
                real = chain[lines, block * whole : block * whole + half]
                imag = chain[lines, block * whole + half : (block + 1) * whole]
                top = line * whole
                right_chain[k, block, top : top + half, :half] = real
                right_chain[k, block, top : top + half, half:] = imag
                right_chain[k, block, top + half : top + whole, :half] = -imag
                right_chain[k, block, top + half : top + whole, half:] = real

    def build_green(k, block):
        for line in range(2):
            real = blocks[2 * line + block, k, 0]
            imag = blocks[2 * line + block, k, 1]
            top = line * whole
            right_green[top : top + half, :half] = real
            right_green[top : top + half, half:] = imag
            right_green[top + half : top + whole, :half] = -imag
            right_green[top + half : top + whole, half:] = real

    build_chain(0)

    per_row = 2 * states_count
    shift = per_row.bit_length() - 1
    shape = (rows_size * per_row, contacts * per_row)
    line_ids = lax.broadcasted_iota(jnp.int32, shape, 0)
    lane_ids = lax.broadcasted_iota(jnp.int32, shape, 1)
    lane_contact = lane_ids >> shift
    lane_row = jnp.zeros(shape, jnp.int32)
    for contact in range(contacts):
        lane_row = jnp.where(lane_contact == contact, contact_ref[contact], lane_row)
    chosen = lane_row == (line_ids >> shift)
    line_item = line_ids & (per_row - 1)
    lane_item = lane_ids & (per_row - 1)
    flat_states = states_ref[...].reshape(contacts * per_row, whole)
    straight = jnp.where(chosen & (line_item == lane_item), 1.0, 0.0).astype(BF16)
    turned_item = (line_item + states_count) & (per_row - 1)
    sign = jnp.where(line_item < states_count, -1.0, 1.0)
    turned = jnp.where(chosen & (turned_item == lane_item), sign, 0.0).astype(BF16)
    drive_straight = mul(straight, flat_states).astype(BF16)
    drive_turned = mul(turned, flat_states).astype(BF16)
    for block in range(2):
        lanes = slice(block * half, (block + 1) * half)
        drive[:, block * whole : block * whole + half] = drive_straight[:, lanes]
        drive[:, block * whole + half : (block + 1) * whole] = drive_turned[:, lanes]

    load_inverse.wait()
    for k in range(iters):
        last = k == iters - 1
        lines = strip if last else slice(0, whole)
        cross[k].wait_recv()
        relay[k].start()
        if k + 2 < iters:
            core[k + 2].start()
        for part in range(2):
            block = column_bit if part == 0 else 1 - column_bit
            if part == 1:
                core[k].wait_recv()
                relay[k].wait_recv()
            build_green(k, block)
            lanes = pl.ds(pl.multiple_of(block * whole, whole), whole)
            product[k, lines, lanes] = mul(chain[lines, :], right_green[...]).astype(BF16)

        @pl.when(column_bit == 0)
        def _():
            share[k].start()

        for block in range(2):
            result = mul(product[k, lines, :], right_chain[k, block]).astype(BF16)
            if last:
                stage[block, 0] = result[:, :half]
                stage[block, 1] = result[:, half:]
            else:
                chain[:, block * whole : (block + 1) * whole] = result
        if last:
            forward_out = remote(
                stage.at[1], far_forward_ref.at[0], far_sems.at[0], far_sems.at[1], "rows", beside
            )
            backward_out = remote(
                stage.at[0], far_backward_ref.at[0], far_sems.at[0], far_sems.at[1], "rows", beside
            )
            forward_keep = pltpu.make_async_copy(
                stage.at[0], far_forward_ref.at[0], local_sems.at[2]
            )
            backward_keep = pltpu.make_async_copy(
                stage.at[1], far_backward_ref.at[0], local_sems.at[2]
            )

            @pl.when(column_bit == 0)
            def _():
                forward_out.start()
                forward_keep.start()

            @pl.when(column_bit == 1)
            def _():
                backward_out.start()
                backward_keep.start()
        else:
            build_chain(k + 1)

        @pl.when(column_bit == 1)
        def _():
            share[k].wait_recv()
            for block in range(2):
                lanes = slice(block * whole, (block + 1) * whole)
                term = mul(arrived[k], right_chain[k, block])
                if k == 0:
                    surface[:, lanes] = term
                else:
                    surface[:, lanes] += term

    def piece(target, send_sem):
        begin = pl.multiple_of(target * per_row, per_row)
        return remote(
            pieces.at[pl.ds(begin, per_row)],
            gathered.at[slot, row_bit],
            send_sem,
            piece_recv.at[2 * slot + row_bit],
            "rows",
            target,
        )

    @pl.when(column_bit == 1)
    def _():
        self_energy = surface[...].astype(BF16)
        pieces[...] = lax.dot_general(
            drive[...], self_energy, (((1,), (1,)), ((), ())), preferred_element_type=F32
        ).astype(BF16)
        for step in range(1, rows_size):
            piece(lax.rem(position + step, rows_size), piece_send.at[step]).start()
        begin = pl.multiple_of(position * per_row, per_row)
        keep = pltpu.make_async_copy(
            pieces.at[pl.ds(begin, per_row)], gathered.at[slot, row_bit], piece_send.at[0]
        )
        keep.start()
        keep.wait()

    for index in range(2 * groups):
        sender = index // 2 * 4 + index % 2 * 2 + 1

        @pl.when(position != sender)
        def _():
            remote(
                pieces.at[pl.ds(0, per_row)],
                gathered.at[index // 2, index % 2],
                piece_send.at[0],
                piece_recv.at[index],
                "rows",
                position,
            ).wait_recv()

    for line in range(2):
        columns = slice(line * half, (line + 1) * half)
        terms = [gathered[index, line].astype(F32) for index in range(groups)]
        total = jnp.zeros_like(terms[0])
        for group in range(groups):
            picked = jnp.zeros_like(total)
            for index in range(groups):
                mark = jnp.full(total.shape, lax.rem(assignment_ref[index], groups), jnp.int32)
                picked = jnp.where(mark == group, terms[index], picked)
            injection_ref[group, 0, :, :, columns] = picked.reshape(2, states_count, half)
            total = total + weights_ref[group] * picked
        weighted[:, columns] = total.astype(BF16)
        over_energy[energy, :, columns] = total.astype(BF16)

    sums = [
        remote(
            weighted,
            over_energy.at[energy],
            energy_send.at[step],
            energy_recv.at[energy],
            "energy",
            lax.rem(energy + step, energy_size),
        )
        for step in range(1, energy_size)
    ]
    for copy in sums:
        copy.start()
    for index in range(energy_size):

        @pl.when(energy != index)
        def _():
            remote(
                weighted,
                over_energy.at[index],
                energy_send.at[0],
                energy_recv.at[index],
                "energy",
                energy,
            ).wait_recv()

    for line in range(2):
        columns = slice(line * half, (line + 1) * half)
        total = over_energy[0, :, columns].astype(F32)
        for index in range(1, energy_size):
            total = total + over_energy[index, :, columns].astype(F32)
        integrated_ref[0, :, :, columns] = total.reshape(2, states_count, half)

    for copy in sums:
        copy.wait_send()
    for k in range(iters):
        cross[k].wait_send()
        core[k].wait_send()
        relay[k].wait_send()

    @pl.when(column_bit == 0)
    def _():
        for k in range(iters):
            share[k].wait_send()
        forward_keep.wait()
        forward_out.wait_send()
        backward_out.wait_recv()

    @pl.when(column_bit == 1)
    def _():
        for step in range(1, rows_size):
            piece(lax.rem(position + step, rows_size), piece_send.at[step]).wait_send()
        backward_keep.wait()
        backward_out.wait_send()
        forward_out.wait_recv()


def local(rows_size, energy_size, coupling, inverses, contact_row, assignment, states, weights):
    iters, half = inverses.shape[1], inverses.shape[-1]
    whole = 2 * half
    groups = assignment.shape[0]
    contacts, _, states_count, _ = states.shape
    per_row = 2 * states_count
    any_space = pl.BlockSpec(memory_space=pl.ANY)
    smem = pl.BlockSpec(memory_space=pltpu.SMEM)
    vmem = pl.BlockSpec(memory_space=pltpu.VMEM)
    dma = pltpu.SemaphoreType.DMA
    far = jax.ShapeDtypeStruct((1, 2, half, half), BF16)
    return pl.pallas_call(
        functools.partial(kernel, rows_size, energy_size),
        out_shape=(
            jax.ShapeDtypeStruct((groups, 1, 2, states_count, whole), F32),
            jax.ShapeDtypeStruct((1, 2, states_count, whole), F32),
            far,
            far,
        ),
        in_specs=[any_space, any_space, smem, smem, vmem, smem],
        out_specs=(vmem, vmem, any_space, any_space),
        scratch_shapes=[
            pltpu.VMEM((2, whole, whole), BF16),
            pltpu.VMEM((4, iters, 2, half, half), BF16),
            pltpu.VMEM((whole, 2 * whole), BF16),
            pltpu.VMEM((iters, whole, 2 * whole), BF16),
            pltpu.VMEM((iters, 2, 2 * whole, whole), BF16),
            pltpu.VMEM((2 * whole, whole), BF16),
            pltpu.VMEM((iters, half, 2 * whole), BF16),
            pltpu.VMEM((half, 2 * whole), F32),
            pltpu.VMEM((rows_size * per_row, 2 * whole), BF16),
            pltpu.VMEM((rows_size * per_row, half), BF16),
            pltpu.VMEM((groups, 2, per_row, half), BF16),
            pltpu.VMEM((per_row, whole), BF16),
            pltpu.VMEM((energy_size, per_row, whole), BF16),
            pltpu.VMEM((2, 2, half, half), BF16),
            dma((3,)),
            dma((2, iters)),
            dma((2, iters)),
            dma((2, iters)),
            dma((2, iters)),
            dma((2,)),
            dma((rows_size,)),
            dma((2 * groups,)),
            dma((energy_size,)),
            dma((energy_size,)),
        ],
        compiler_params=pltpu.CompilerParams(
            collective_id=0, has_side_effects=True, vmem_limit_bytes=60 * 1024 * 1024
        ),
        name="decimate",
    )(coupling, inverses, contact_row, assignment, states, weights)


def solution(mesh):
    rows_size, energy_size = mesh.shape["rows"], mesh.shape["energy"]
    placed = (
        P(),
        P(("energy", "rows"), None, None, None, None),
        P(),
        P("energy"),
        P(),
        P("energy"),
    )
    return jax.shard_map(
        functools.partial(local, rows_size, energy_size),
        mesh=mesh,
        in_specs=placed,
        out_specs=(
            P("energy", "rows", None, None, None),
            P("rows", None, None, None),
            P(("energy", "rows"), None, None, None),
            P(("energy", "rows"), None, None, None),
        ),
        check_vma=False,
    )
```

time: 176 us -> 48.8 us (0.28)
  matrix products: 88.4 us -> 0 us
  Pallas kernels: 0 us -> 43.1 us
  starting transfers between devices: 32.4 us -> 0 us
  blocking collectives: 19.3 us -> 0 us
  waiting for transfers between devices: 14.4 us -> 0 us
  local copies, waits for them, and re-layouts: 11.5 us -> 4.83 us
  other arithmetic: 5.75 us -> 0 us
    dot_general x166 -> x0, matrix products: 88.4 us -> none  [the longest x160 85 us: single(): return jnp.dot(leading, trailing, preferred_element_type=jnp.float32)]
    pallas_call x0 -> x1, Pallas kernels: none -> 43.1 us  [local(): pl.pallas_call(functools.partial(kernel, rows_size, energy_size), out_sha...]
    ppermute x28 -> x0, starting transfers between devices: 25.5 us -> none  [partner(): lax.ppermute(shard, axis, [(i, i ^ 1 << stride) for i in range(lax.axis_s...]
    psum x1 -> x0, blocking collectives: 19.3 us -> none  [local(): lax.psum(weighted.astype(jnp.bfloat16), 'energy').astype(jnp.float32)]
    ppermute x28 -> x0, waiting for transfers between devices: 14.4 us -> none  [partner(): lax.ppermute(shard, axis, [(i, i ^ 1 << stride) for i in range(lax.axis_s...]
    all_to_all x1 -> x0, starting transfers between devices: 6.89 us -> none  [local(): lax.all_to_all(partial_terms[:, None].astype(jnp.bfloat16), 'rows', split...]
    dynamic_slice x3 -> x0, local copies, waits for them, and re-layouts: 3.5 us -> none  [the longest x2 2.51 us: local(): lax.dynamic_index_in_dim(drive, column_bit, axis=3, keepdims=False)]
    another operation x23 -> x0, other arithmetic: 2.95 us -> none  [the longest x20 2.89 us: paired_dot(): return jnp.stack([real_part, imag_part])]
  transfers between devices with their start and end apart: 29 -> 0, of which waited for: 4 -> 0; matrix products, arithmetic and copies ran while one was open for 57% -> 0% of each run, Pallas kernels for 0% -> 0%
where the time goes in v1:
time: 48.8 us; the launch traced here: 48.6 us
  Pallas kernels  43.1 us (88%)
  local copies, waits for them, and re-layouts  4.83 us (10%)
  between operations  0.65 us (1%)
    pallas_call x1, Pallas kernels, local(): pl.pallas_call(functools.partial(kernel, rows_size, energy_size), out_sha...  43.1 us
    unnamed x8, local copies, waits for them, and re-layouts  4.83 us

profile of v1, /device:TPU:0, one launch (start us, length us, event | category | flops | bytes accessed | tf_op | source)
XLA Modules:
  0.0 48.6 jit_solution(8312279821736070122)
XLA Ops:
  0.6 43.1 %decimate.1 = (f32[2,1,2,16,512]{4,3,2,1,0:T(8,128)}, f32[1,2,16,512]{3,2,1,0:T(8,128)}, bf16[1,2,256,256]{3,2,1,0:T(8,128)(2,1)}, bf16[1,2,256,256]{3,2,1,0:T(8,128)(2,1)}) custom-call(bf16[2,512,512]{2,1,0:T(8,128)(2,1)} %coupling_ref.1, bf16[1,4,2,256,256]{4,3,2,1,0:T(8,128)(2,1)} %inverses_ref.1, s32[12]{0:T(128)} %contact_ref.1, s32[2]{0:T(128)} %assignment_ref.1, ...), custom_call_target="tpu_custom_call" | custom-call | tf_op jit(solution)/shard_map/decimate/pallas_call | solution.py:410
  43.7 0.0 copy-start.1
  43.7 1.6 %copy.14 = f32[2,1,2,16,512]{4,3,2,1,0:T(8,128)} copy(f32[2,1,2,16,512]{4,3,2,1,0:T(8,128)} %get-tuple-element.8) | data formatting | bytes 262144
  45.3 1.5 %copy.15 = f32[1,2,16,512]{3,2,1,0:T(8,128)} copy(f32[1,2,16,512]{3,2,1,0:T(8,128)} %get-tuple-element.9) | data formatting | bytes 131072
  46.8 0.0 copy-done.1
  46.8 0.0 copy-start
  46.8 0.7 %copy.16 = bf16[1,2,256,256]{3,2,1,0:T(8,128)(2,1)} copy(bf16[1,2,256,256]{3,2,1,0:T(8,128)(2,1)S(1)} %copy-done.1) | data formatting | bytes 524288
  47.5 0.3 copy-done
  47.9 0.7 %copy.17 = bf16[1,2,256,256]{3,2,1,0:T(8,128)(2,1)} copy(bf16[1,2,256,256]{3,2,1,0:T(8,128)(2,1)S(1)} %copy-done) | data formatting | bytes 524288
Async XLA Ops:
  43.7 3.1 %copy-start.1 = (bf16[1,2,256,256]{3,2,1,0:T(8,128)(2,1)S(1)}, bf16[1,2,256,256]{3,2,1,0:T(8,128)(2,1)}, u32[]{:S(2)}) copy-start(bf16[1,2,256,256]{3,2,1,0:T(8,128)(2,1)} %get-tuple-element.10) | copy-start | bytes 786436
  46.8 1.0 %copy-start = (bf16[1,2,256,256]{3,2,1,0:T(8,128)(2,1)S(1)}, bf16[1,2,256,256]{3,2,1,0:T(8,128)(2,1)}, u32[]{:S(2)}) copy-start(bf16[1,2,256,256]{3,2,1,0:T(8,128)(2,1)} %get-tuple-element.11) | copy-start | bytes 786436

commit v2 on v1

--- a/solution.py
+++ b/solution.py
@@ -48,6 +48,11 @@
     right_green,
     arrived,
     surface,
+    side,
+    left_green,
+    right_term,
+    total_surface,
+    states_held,
     drive,
     pieces,
     gathered,
@@ -86,6 +91,8 @@
         inverses_ref.at[0], blocks.at[own_block], local_sems.at[1]
     )
     load_inverse.start()
+    load_states = pltpu.make_async_copy(states_ref, states_held, local_sems.at[3])
+    load_states.start()
 
     barrier = pltpu.get_barrier_semaphore()
     for step in range(1, rows_size):
@@ -137,11 +144,12 @@
         )
         for k in range(iters)
     ]
+    side_lanes = pl.ds(pl.multiple_of(row_bit * whole, whole), whole)
     strip = pl.ds(pl.multiple_of(row_bit * half, half), half)
     share = [
         remote(
-            product.at[k, strip],
-            arrived.at[k],
+            product.at[k, strip] if k < iters - 1 else chain.at[:, side_lanes],
+            arrived.at[k] if k < iters - 1 else side,
             product_sems.at[0, k],
             product_sems.at[1, k],
             "rows",
@@ -208,7 +216,8 @@
     chosen = lane_row == (line_ids >> shift)
     line_item = line_ids & (per_row - 1)
     lane_item = lane_ids & (per_row - 1)
-    flat_states = states_ref[...].reshape(contacts * per_row, whole)
+    load_states.wait()
+    flat_states = states_held[...].reshape(contacts * per_row, whole)
     straight = jnp.where(chosen & (line_item == lane_item), 1.0, 0.0).astype(BF16)
     turned_item = (line_item + states_count) & (per_row - 1)
     sign = jnp.where(line_item < states_count, -1.0, 1.0)
@@ -220,10 +229,108 @@
         drive[:, block * whole : block * whole + half] = drive_straight[:, lanes]
         drive[:, block * whole + half : (block + 1) * whole] = drive_turned[:, lanes]
 
+    def piece(target, send_sem):
+        begin = pl.multiple_of(target * per_row, per_row)
+        return remote(
+            pieces.at[pl.ds(begin, per_row)],
+            gathered.at[slot, row_bit],
+            send_sem,
+            piece_recv.at[2 * slot + row_bit],
+            "rows",
+            target,
+        )
+
+    def finish_surface():
+        k = iters - 1
+        core[k].wait_recv()
+        pl.when(column_bit == 1)(close_surface)
+
+    def close_surface():
+        k = iters - 1
+        for block in range(2):
+            for index in range(2):
+                lanes = slice(block * whole + index * half, block * whole + (index + 1) * half)
+                left_green[:, lanes] = blocks[2 * row_bit + block, k, index]
+        for block in range(2):
+            term = mul(left_green[...], right_chain[k, block]).astype(BF16)
+            real, imag = term[:, :half], term[:, half:]
+            right_term[block, :half, :half] = real
+            right_term[block, :half, half:] = imag
+            right_term[block, half:, :half] = -imag
+            right_term[block, half:, half:] = real
+        share[k].wait_recv()
+        for line in range(2):
+            lines = slice(line * half, (line + 1) * half)
+            for block in range(2):
+                lanes = slice(block * whole, (block + 1) * whole)
+                term = mul(side[lines, :], right_term[block])
+                before = jnp.where(row_bit == line, surface[:, lanes], 0.0)
+                total_surface[lines, lanes] = (term + before).astype(BF16)
+        pieces[...] = lax.dot_general(
+            drive[...], total_surface[...], (((1,), (1,)), ((), ())), preferred_element_type=F32
+        ).astype(BF16)
+        for step in range(1, rows_size):
+            piece(lax.rem(position + step, rows_size), piece_send.at[step]).start()
+        begin = pl.multiple_of(position * per_row, per_row)
+        keep = pltpu.make_async_copy(
+            pieces.at[pl.ds(begin, per_row)], gathered.at[slot, row_bit], piece_send.at[0]
+        )
+        keep.start()
+        keep.wait()
+
+    def gather():
+        for index in range(2 * groups):
+            sender = index // 2 * 4 + index % 2 * 2 + 1
+
+            @pl.when(position != sender)
+            def _():
+                remote(
+                    pieces.at[pl.ds(0, per_row)],
+                    gathered.at[index // 2, index % 2],
+                    piece_send.at[0],
+                    piece_recv.at[index],
+                    "rows",
+                    position,
+                ).wait_recv()
+
+        for line in range(2):
+            columns = slice(line * half, (line + 1) * half)
+            terms = [
+                gathered[index, 0, :, columns].astype(F32) + gathered[index, 1, :, columns].astype(F32)
+                for index in range(groups)
+            ]
+            total = jnp.zeros_like(terms[0])
+            for group in range(groups):
+                picked = jnp.zeros_like(total)
+                for index in range(groups):
+                    mark = jnp.full(total.shape, lax.rem(assignment_ref[index], groups), jnp.int32)
+                    picked = jnp.where(mark == group, terms[index], picked)
+                injection_ref[group, 0, :, :, columns] = picked.reshape(2, states_count, half)
+                total = total + weights_ref[group] * picked
+            weighted[:, columns] = total.astype(BF16)
+            over_energy[energy, :, columns] = total.astype(BF16)
+
+        sums = [
+            remote(
+                weighted,
+                over_energy.at[energy],
+                energy_send.at[step],
+                energy_recv.at[energy],
+                "energy",
+                lax.rem(energy + step, energy_size),
+            )
+            for step in range(1, energy_size)
+        ]
+        for copy in sums:
+            copy.start()
+        return sums
+
     load_inverse.wait()
     for k in range(iters):
         last = k == iters - 1
         lines = strip if last else slice(0, whole)
+        if last:
+            finish_surface()
         cross[k].wait_recv()
         relay[k].start()
         if k + 2 < iters:
@@ -231,16 +338,21 @@
         for part in range(2):
             block = column_bit if part == 0 else 1 - column_bit
             if part == 1:
-                core[k].wait_recv()
+                if not last:
+                    core[k].wait_recv()
                 relay[k].wait_recv()
             build_green(k, block)
             lanes = pl.ds(pl.multiple_of(block * whole, whole), whole)
             product[k, lines, lanes] = mul(chain[lines, :], right_green[...]).astype(BF16)
 
-        @pl.when(column_bit == 0)
-        def _():
-            share[k].start()
-
+        if not last:
+
+            @pl.when(column_bit == 0)
+            def _():
+                share[k].start()
+
+        if last:
+            sums = gather()
         for block in range(2):
             result = mul(product[k, lines, :], right_chain[k, block]).astype(BF16)
             if last:
@@ -272,86 +384,25 @@
                 backward_out.start()
                 backward_keep.start()
         else:
+            if k == iters - 2:
+
+                @pl.when(column_bit == 0)
+                def _():
+                    share[k + 1].start()
+
             build_chain(k + 1)
 
-        @pl.when(column_bit == 1)
-        def _():
-            share[k].wait_recv()
-            for block in range(2):
-                lanes = slice(block * whole, (block + 1) * whole)
-                term = mul(arrived[k], right_chain[k, block])
-                if k == 0:
-                    surface[:, lanes] = term
-                else:
-                    surface[:, lanes] += term
-
-    def piece(target, send_sem):
-        begin = pl.multiple_of(target * per_row, per_row)
-        return remote(
-            pieces.at[pl.ds(begin, per_row)],
-            gathered.at[slot, row_bit],
-            send_sem,
-            piece_recv.at[2 * slot + row_bit],
-            "rows",
-            target,
-        )
-
-    @pl.when(column_bit == 1)
-    def _():
-        self_energy = surface[...].astype(BF16)
-        pieces[...] = lax.dot_general(
-            drive[...], self_energy, (((1,), (1,)), ((), ())), preferred_element_type=F32
-        ).astype(BF16)
-        for step in range(1, rows_size):
-            piece(lax.rem(position + step, rows_size), piece_send.at[step]).start()
-        begin = pl.multiple_of(position * per_row, per_row)
-        keep = pltpu.make_async_copy(
-            pieces.at[pl.ds(begin, per_row)], gathered.at[slot, row_bit], piece_send.at[0]
-        )
-        keep.start()
-        keep.wait()
-
-    for index in range(2 * groups):
-        sender = index // 2 * 4 + index % 2 * 2 + 1
-
-        @pl.when(position != sender)
-        def _():
-            remote(
-                pieces.at[pl.ds(0, per_row)],
-                gathered.at[index // 2, index % 2],
-                piece_send.at[0],
-                piece_recv.at[index],
-                "rows",
-                position,
-            ).wait_recv()
-
-    for line in range(2):
-        columns = slice(line * half, (line + 1) * half)
-        terms = [gathered[index, line].astype(F32) for index in range(groups)]
-        total = jnp.zeros_like(terms[0])
-        for group in range(groups):
-            picked = jnp.zeros_like(total)
-            for index in range(groups):
-                mark = jnp.full(total.shape, lax.rem(assignment_ref[index], groups), jnp.int32)
-                picked = jnp.where(mark == group, terms[index], picked)
-            injection_ref[group, 0, :, :, columns] = picked.reshape(2, states_count, half)
-            total = total + weights_ref[group] * picked
-        weighted[:, columns] = total.astype(BF16)
-        over_energy[energy, :, columns] = total.astype(BF16)
-
-    sums = [
-        remote(
-            weighted,
-            over_energy.at[energy],
-            energy_send.at[step],
-            energy_recv.at[energy],
-            "energy",
-            lax.rem(energy + step, energy_size),
-        )
-        for step in range(1, energy_size)
-    ]
-    for copy in sums:
-        copy.start()
+            @pl.when(column_bit == 1)
+            def _():
+                share[k].wait_recv()
+                for block in range(2):
+                    lanes = slice(block * whole, (block + 1) * whole)
+                    term = mul(arrived[k], right_chain[k, block])
+                    if k == 0:
+                        surface[:, lanes] = term
+                    else:
+                        surface[:, lanes] += term
+
     for index in range(energy_size):
 
         @pl.when(energy != index)
@@ -396,6 +447,19 @@
         forward_out.wait_recv()
 
 
+def deliver(*refs):
+    count = len(refs) // 2
+    sems = refs[-1]
+    copies = [
+        pltpu.make_async_copy(refs[index], refs[count + index], sems.at[index])
+        for index in range(count)
+    ]
+    for copy in copies:
+        copy.start()
+    for copy in copies:
+        copy.wait()
+
+
 def local(rows_size, energy_size, coupling, inverses, contact_row, assignment, states, weights):
     iters, half = inverses.shape[1], inverses.shape[-1]
     whole = 2 * half
@@ -403,11 +467,16 @@
     contacts, _, states_count, _ = states.shape
     per_row = 2 * states_count
     any_space = pl.BlockSpec(memory_space=pl.ANY)
+    hbm = pl.BlockSpec(memory_space=pltpu.HBM)
     smem = pl.BlockSpec(memory_space=pltpu.SMEM)
     vmem = pl.BlockSpec(memory_space=pltpu.VMEM)
     dma = pltpu.SemaphoreType.DMA
     far = jax.ShapeDtypeStruct((1, 2, half, half), BF16)
-    return pl.pallas_call(
+    coupling, inverses, contact_row, assignment, states, weights = (
+        pltpu.with_memory_space_constraint(item, pltpu.HBM)
+        for item in (coupling, inverses, contact_row, assignment, states, weights)
+    )
+    outputs = pl.pallas_call(
         functools.partial(kernel, rows_size, energy_size),
         out_shape=(
             jax.ShapeDtypeStruct((groups, 1, 2, states_count, whole), F32),
@@ -415,7 +484,7 @@
             far,
             far,
         ),
-        in_specs=[any_space, any_space, smem, smem, vmem, smem],
+        in_specs=[hbm, hbm, smem, smem, hbm, smem],
         out_specs=(vmem, vmem, any_space, any_space),
         scratch_shapes=[
             pltpu.VMEM((2, whole, whole), BF16),
@@ -424,15 +493,20 @@
             pltpu.VMEM((iters, whole, 2 * whole), BF16),
             pltpu.VMEM((iters, 2, 2 * whole, whole), BF16),
             pltpu.VMEM((2 * whole, whole), BF16),
-            pltpu.VMEM((iters, half, 2 * whole), BF16),
+            pltpu.VMEM((iters - 1, half, 2 * whole), BF16),
             pltpu.VMEM((half, 2 * whole), F32),
+            pltpu.VMEM((whole, whole), BF16),
+            pltpu.VMEM((half, 2 * whole), BF16),
+            pltpu.VMEM((2, whole, whole), BF16),
+            pltpu.VMEM((whole, 2 * whole), BF16),
+            pltpu.VMEM(states.shape, BF16),
             pltpu.VMEM((rows_size * per_row, 2 * whole), BF16),
-            pltpu.VMEM((rows_size * per_row, half), BF16),
-            pltpu.VMEM((groups, 2, per_row, half), BF16),
+            pltpu.VMEM((rows_size * per_row, whole), BF16),
+            pltpu.VMEM((groups, 2, per_row, whole), BF16),
             pltpu.VMEM((per_row, whole), BF16),
             pltpu.VMEM((energy_size, per_row, whole), BF16),
             pltpu.VMEM((2, 2, half, half), BF16),
-            dma((3,)),
+            dma((4,)),
             dma((2, iters)),
             dma((2, iters)),
             dma((2, iters)),
@@ -444,10 +518,19 @@
             dma((energy_size,)),
         ],
         compiler_params=pltpu.CompilerParams(
-            collective_id=0, has_side_effects=True, vmem_limit_bytes=60 * 1024 * 1024
+            collective_id=0, has_side_effects=True, vmem_limit_bytes=36 * 1024 * 1024
         ),
         name="decimate",
     )(coupling, inverses, contact_row, assignment, states, weights)
+    return pl.pallas_call(
+        deliver,
+        out_shape=tuple(jax.ShapeDtypeStruct(item.shape, item.dtype) for item in outputs),
+        in_specs=[vmem] * len(outputs),
+        out_specs=(hbm,) * len(outputs),
+        scratch_shapes=[dma((len(outputs),))],
+        compiler_params=pltpu.CompilerParams(vmem_limit_bytes=8 * 1024 * 1024),
+        name="deliver",
+    )(*outputs)
 
 
 def solution(mesh):

time: 48.8 us -> 41.4 us (0.85)
  local copies, waits for them, and re-layouts: 4.83 us -> 0 us
  Pallas kernels: 43.1 us -> 40.6 us
    unnamed x8 -> x0, local copies, waits for them, and re-layouts: 4.83 us -> none
    pallas_call x1, Pallas kernels: 43.1 us -> 39.7 us  [local(): pl.pallas_call(functools.partial(kernel, rows_size, energy_size), out_sha...]
    pallas_call x0 -> x1, Pallas kernels: none -> 0.89 us  [local(): pl.pallas_call(deliver, out_shape=tuple((jax.ShapeDtypeStruct(item.shape,...]
where the time goes in v2:
time: 41.4 us; the launch traced here: 41.2 us
  Pallas kernels  40.6 us (98%)
  between operations  0.64 us (2%)
    pallas_call x1, Pallas kernels, local(): pl.pallas_call(functools.partial(kernel, rows_size, energy_size), out_sha...  39.7 us
    pallas_call x1, Pallas kernels, local(): pl.pallas_call(deliver, out_shape=tuple((jax.ShapeDtypeStruct(item.shape,...  0.89 us

profile of v2, /device:TPU:0, one launch (start us, length us, event | category | flops | bytes accessed | tf_op | source)
XLA Modules:
  0.0 41.2 jit_solution(7811257133203269337)
XLA Ops:
  0.6 39.7 %decimate.1 = (f32[2,1,2,16,512]{4,3,2,1,0:T(8,128)S(1)}, f32[1,2,16,512]{3,2,1,0:T(8,128)S(1)}, bf16[1,2,256,256]{3,2,1,0:T(8,128)(2,1)S(1)}, bf16[1,2,256,256]{3,2,1,0:T(8,128)(2,1)S(1)}) custom-call(bf16[2,512,512]{2,1,0:T(8,128)(2,1)} %coupling_ref.1, bf16[1,4,2,256,256]{4,3,2,1,0:T(8,128)(2,1)} %inverses_ref.1, s32[12]{0:T(128)} %contact_ref.1, ...), custom_call_target="tpu_custom_call" | custom-call | tf_op jit(solution)/shard_map/decimate/pallas_call | solution.py:479
  40.3 0.9 %deliver.1 = (f32[2,1,2,16,512]{4,3,2,1,0:T(8,128)}, f32[1,2,16,512]{3,2,1,0:T(8,128)}, bf16[1,2,256,256]{3,2,1,0:T(8,128)(2,1)}, bf16[1,2,256,256]{3,2,1,0:T(8,128)(2,1)}) custom-call(f32[2,1,2,16,512]{4,3,2,1,0:T(8,128)S(1)} %get-tuple-element.8.refs_0_, f32[1,2,16,512]{3,2,1,0:T(8,128)S(1)} %get-tuple-element.9.refs_1_, ...), custom_call_target="tpu_custom_call" | custom-call | tf_op jit(solution)/shard_map/deliver/pallas_call | solution.py:525
